TPU v7x, 256 devices: a whole 4x4x8 slice. The times are simulated.
256 devices in a mesh: stn: 64 (over y_hi, z, x), beam: 4 (over y_lo, core).
Axes of the slice: x: 4, y: 4 (y_hi: 2, y_lo: 2; y = y_hi * 2 + y_lo), z: 8, core: 2. Of those that a mesh axis runs over, the one named last changes fastest.
Arguments:
- voltages: bfloat16 [512, 2, 614400], P(('stn', 'beam')), may hold values from -6 to 6
- fir_taps: float32 [12, 8192], replicated, may hold values from -1.75 to 1.75
- delays: float32 [64, 64, 512], P('stn', 'beam'), may hold values from -16 to 16
- taper: float32 [64, 512], replicated, may hold values from 0.5 to 2
- station_map: int32 [512], replicated, may hold values from 0 to 511, each once
- beam_order: int32 [64], replicated, may hold values from 0 to 63, each once
- owners: int32 [4], replicated, may hold values from 0 to 63
Outputs:
- beams_re: float32 [64, 4096, 128], P('beam', 'stn')
- beams_im: float32 [64, 4096, 128], P('beam', 'stn')
Inputs may be any that keep to these rules, and one draw needn't show every extreme that they name: `station_map`: each station row holds a different physical station. `beam_order`: each beam slot forms a different beam.
All inputs are finite; a program needn't handle non-finite values.
Results may differ from a plain program's by a relative error of at most 0.0064.
Values may be sent and summed in bfloat16 or wider, within the bound.
No kernel may reach another device: no remote copies, remote signals or barrier semaphores. Data moves between devices by JAX's collectives and lax.ppermute only.
A program may use at most 128 MiB of HBM per device.

v0:
```python
import math
import jax
import jax.numpy as jnp
from jax import lax
from jax.sharding import PartitionSpec as P

P_SIZE = 64
Q = 128
CHANNELS = 4096
TWO_PI = 2.0 * math.pi


def from_root(value, axis, source):
    kept = jnp.where(lax.axis_index(axis) == source, value, 0).astype(value.dtype)
    return lax.psum(kept, axis)


def dft_tables():
    first_idx = jnp.arange(P_SIZE, dtype=jnp.int32)
    second_idx = jnp.arange(Q, dtype=jnp.int32)
    half_idx = jnp.arange(Q // 2, dtype=jnp.int32)
    first_angle = (
        TWO_PI / P_SIZE * (first_idx[:, None] * first_idx[None, :] % P_SIZE).astype(jnp.float32)
    )
    twist_angle = (
        TWO_PI / (P_SIZE * Q) * (first_idx[:, None] * second_idx[None, :]).astype(jnp.float32)
    )
    second_angle = TWO_PI / Q * (second_idx[:, None] * half_idx[None, :] % Q).astype(jnp.float32)
    return (
        jnp.cos(first_angle).astype(jnp.bfloat16),
        jnp.sin(first_angle).astype(jnp.bfloat16),
        jnp.cos(twist_angle),
        jnp.sin(twist_angle),
        jnp.cos(second_angle).astype(jnp.bfloat16),
        jnp.sin(second_angle).astype(jnp.bfloat16),
    )


def beam_weights(delay_cols, gain_cols, chan_ids):
    phase = (
        delay_cols[:, :, None]
        * chan_ids.astype(jnp.float32)[None, None, :]
        * (TWO_PI / (P_SIZE * Q))
    )
    weight_re = (gain_cols[:, :, None] * jnp.cos(phase)).astype(jnp.bfloat16)
    weight_im = (-(gain_cols[:, :, None] * jnp.sin(phase))).astype(jnp.bfloat16)
    left_re = jnp.concatenate((weight_re, -weight_im), axis=1)
    left_im = jnp.concatenate((weight_im, weight_re), axis=1)
    return (left_re, left_im)


def channelize(voltages, fir_taps):
    cos_one, sin_one, twist_cos, twist_sin, cos_two, sin_two = dft_tables()
    local_stations, pol_count, samples = voltages.shape
    tap_count, fft_width = fir_taps.shape
    frames = samples // fft_width - tap_count + 1
    blocks = voltages.reshape(local_stations, pol_count, frames + tap_count - 1, fft_width)
    filtered = jnp.zeros((local_stations, pol_count, frames, fft_width), jnp.float32)
    for tap_idx in range(tap_count):
        filtered = filtered + fir_taps[tap_idx] * blocks[:, :, tap_idx : tap_idx + frames].astype(
            jnp.float32
        )
    folded = filtered.astype(jnp.bfloat16).reshape(local_stations, pol_count, frames, P_SIZE, Q)
    first_table = jnp.concatenate((cos_one, -sin_one), axis=0)
    first_section = jnp.einsum(
        "spfnq,an->spfaq", folded, first_table, preferred_element_type=jnp.float32
    )
    first_re = first_section[:, :, :, :P_SIZE]
    first_im = first_section[:, :, :, P_SIZE:]
    turned = jnp.concatenate(
        (
            (first_re * twist_cos + first_im * twist_sin).astype(jnp.bfloat16),
            (first_im * twist_cos - first_re * twist_sin).astype(jnp.bfloat16),
        ),
        axis=4,
    )
    second_table = jnp.concatenate(
        (jnp.concatenate((cos_two, -sin_two), axis=1), jnp.concatenate((sin_two, cos_two), axis=1)),
        axis=0,
    )
    second = jnp.einsum("spfaq,qb->sbapf", turned, second_table, preferred_element_type=jnp.float32)
    half_q = Q // 2
    chan_re = (
        second[:, :half_q]
        .astype(jnp.bfloat16)
        .reshape(local_stations, half_q * P_SIZE, pol_count * frames)
    )
    chan_im = (
        second[:, half_q:]
        .astype(jnp.bfloat16)
        .reshape(local_stations, half_q * P_SIZE, pol_count * frames)
    )
    return jnp.stack((chan_re, chan_im), axis=0)


def combine(left_re, left_im, stacked_parts, beam_scale):
    stacked = jnp.concatenate((stacked_parts[0], stacked_parts[1]), axis=0)
    beam_re = (
        jnp.einsum("jrk,rkc->jkc", left_re, stacked, preferred_element_type=jnp.float32)
        * beam_scale
    )
    beam_im = (
        jnp.einsum("jrk,rkc->jkc", left_im, stacked, preferred_element_type=jnp.float32)
        * beam_scale
    )
    return jnp.stack((beam_re, beam_im), axis=0)


def on_device(voltages, fir_taps, delays, taper, station_map, beam_order, owners):
    stn_count = lax.axis_size("stn")
    beam_count = lax.axis_size("beam")
    stn_pos = lax.axis_index("stn")
    beam_pos = lax.axis_index("beam")
    local_stations = voltages.shape[0]
    stations = station_map.shape[0]
    group_beams = beam_order.shape[0] // beam_count
    chan_dev = CHANNELS // stn_count
    chan_ids = stn_pos * chan_dev + jnp.arange(chan_dev, dtype=jnp.int32)
    beam_scale = 1.0 / math.sqrt(P_SIZE * Q * stations)
    spectra = channelize(voltages, fir_taps)
    owner_model = from_root(delays, "stn", owners[beam_pos])[0]
    row_stn = jnp.arange(stn_count * local_stations, dtype=jnp.int32)
    all_rows = (
        (row_stn // local_stations * beam_count + jnp.arange(beam_count, dtype=jnp.int32)[:, None])
        * local_stations
        + row_stn % local_stations
    ).reshape(-1)
    phys_ids = station_map[all_rows]
    slot_gain = taper[beam_order[beam_pos * group_beams + jnp.arange(group_beams, dtype=jnp.int32)]]
    left_re, left_im = beam_weights(owner_model[:, phys_ids], slot_gain[:, phys_ids], chan_ids)
    full_rows = lax.all_gather(
        lax.all_to_all(spectra, "stn", split_axis=2, concat_axis=1, tiled=True),
        "beam",
        axis=1,
        tiled=True,
    )
    formed = combine(left_re, left_im, full_rows, beam_scale)
    return (formed[0], formed[1])


def solution(mesh):
    return jax.shard_map(
        on_device,
        mesh=mesh,
        in_specs=(P(("stn", "beam"), None, None), P(), P("stn", "beam", None), P(), P(), P(), P()),
        out_specs=(P("beam", "stn", None), P("beam", "stn", None)),
        check_vma=False,
    )
```

profile of v0, /device:TPU:16, one launch (start us, length us, event | category | flops | bytes accessed | tf_op | source)
XLA Modules:
  0.0 628.2 jit_solution(1775256071955894884)
XLA Ops:
  7.2 0.0 copy-start
  7.2 0.0 all-gather.2.cloned.1.call-start
  7.2 0.1 cosine_convert_fusion.1
  7.4 0.1 fusion.46
  7.5 0.1 fusion.41
  7.7 0.3 sine_convert_fusion
  7.9 0.3 fusion.49
  8.2 2.6 fusion.59
  10.9 6.3 reshape.166
  17.1 28.3 %add_convert_fusion.1 = bf16[2,2,64,8192]{3,2,1,0:T(8,128)(2,1)S(1)} fusion(bf16[2,2,75,8192]{3,2,1,0:T(8,128)(2,1)} %reshape.166, f32[8192]{0:T(1024)S(1)} %bitcast.83, f32[8192]{0:T(1024)S(1)} %bitcast.84, f32[8192]{0:T(1024)S(1)} %bitcast.74, f32[8192]{0:T(1024)S(1)} %bitcast.75, f32[8192]{0:T(1024)S(1)} %bitcast.76, f32[8192]{0:T(1024)S(1)} %bitcast.77, ...), kind=kLoop, calls=%fused_computation.16 | loop fusion | flops 75497472 | bytes 54919168 | tf_op jit(solution)/shard_map/convert_element_type | solution.py:63
  45.4 1.2 copy.38
  46.6 2.4 convolution_bitcast_fusion
  49.0 2.5 add_convert_fusion
  51.6 3.1 convert_bitcast_fusion
  54.7 4.3 fusion.58
  59.0 6.3 %copy.25 = bf16[2,64,64,2,64]{2,1,4,3,0:T(8,128)(2,1)} copy(bf16[2,64,64,2,64]{1,2,4,3,0:T(8,128)(2,1)} %get-tuple-element.12) | data formatting | bytes 4194304 | tf_op jit(solution)/shard_map/slice | solution.py:84
  65.3 5.7 stack_reshape.6
  71.0 6.4 %copy.26 = bf16[2,64,64,2,64]{2,1,4,3,0:T(8,128)(2,1)} copy(bf16[2,64,64,2,64]{1,2,4,3,0:T(8,128)(2,1)} %get-tuple-element.13) | data formatting | bytes 4194304 | tf_op jit(solution)/shard_map/slice | solution.py:89
  77.3 6.6 %stack_reshape.7 = bf16[1,2,4096,128]{2,3,1,0:T(8,128)(2,1)} reshape(bf16[2,64,64,2,64]{2,1,4,3,0:T(8,128)(2,1)} %copy.26) | data formatting | bytes 4194304 | tf_op jit(solution)/shard_map/stack;reshape | solution.py:93
  83.9 3.9 pad_maximum_fusion.3
  87.8 11.1 %copy.27 = bf16[2,2,4096,128]{3,1,0,2:T(2,128)(2,1)} copy(bf16[2,2,4096,128]{2,3,1,0:T(8,128)(2,1)} %pad_maximum_fusion.3) | data formatting | bytes 8388608 | tf_op jit(solution)/shard_map/stack | solution.py:93
  99.0 108.4 %all_to_all.18 = bf16[2,2,4096,128]{3,1,0,2:T(2,128)(2,1)S(1)} all-to-all(bf16[2,2,4096,128]{3,1,0,2:T(2,128)(2,1)} %copy.27), channel_id=1, replica_groups=mesh['stn'=64,'beam'=4] {'stn'}, dimensions={2} | all-to-all | bytes 8388608 | tf_op jit(solution)/shard_map/all_to_all | solution.py:132
  207.4 2.5 copy.28
  209.9 8.5 %copy.29 = bf16[2,64,2,64,128]{4,2,1,3,0:T(2,128)(2,1)} copy(bf16[2,64,2,64,128]{4,3,1,2,0:T(8,128)(2,1)} %bitcast.69) | data formatting | bytes 8388608 | tf_op jit(solution)/shard_map/all_to_all | solution.py:132
  218.4 0.0 all-gather.2.cloned.1.call-update
  218.4 0.0 copy-done.3
  218.4 0.1 copy.32
  218.5 0.0 copy-done.4
  218.6 0.6 dynamic_slice.3
  219.8 0.0 copy-done.1
  219.9 3.5 gather_fusion.2
  223.4 359.8 %psum.7 = f32[16,512]{0,1:T(8,128)S(1)} all-reduce(f32[16,512]{0,1:T(8,128)S(1)} %select_bitcast_fusion), channel_id=1, replica_groups=mesh['stn'=64,'beam'=4] {'stn'}, use_global_device_ids=true, to_apply=%region_0.1 | all-reduce | flops 8192 | bytes 65536 | tf_op jit(solution)/shard_map/psum | solution.py:15
  583.2 1.0 gather_fusion.4
  584.3 0.1 copy.33
  584.4 0.0 copy-done.2
  584.4 0.7 gather_fusion
  585.1 0.0 copy-done
  585.1 0.6 gather_fusion.1
  585.7 0.1 copy.30
  585.8 1.0 gather_fusion.3
  586.9 0.1 copy.31
  587.0 8.3 %fusion.57 = bf16[16,512,64]{1,0,2:T(8,128)(2,1)} fusion(f32[64]{0:T(128)S(1)} %add_convert_fusion.2, f32[16,512]{1,0:T(8,128)S(1)} %copy.33, f32[16,512]{1,0:T(8,128)S(1)} %copy.31), kind=kLoop, calls=%fused_computation.93 | loop fusion | flops 4194304 | bytes 1114368 | tf_op jit(solution)/shard_map/neg | solution.py:47
  595.3 9.2 %negate_convert_fusion = (bf16[16,512,64]{1,0,2:T(8,128)(2,1)}, bf16[16,512,64]{1,0,2:T(8,128)(2,1)}) fusion(f32[64]{0:T(128)S(1)} %add_convert_fusion.2, f32[16,512]{1,0:T(8,128)S(1)} %copy.33, f32[16,512]{1,0:T(8,128)S(1)} %copy.31), kind=kLoop, calls=%fused_computation.26 | loop fusion | flops 3670016 | bytes 2162944 | tf_op jit(solution)/shard_map/convert_element_type | solution.py:46
  604.5 6.6 %slice_bitcast_fusion.1 = (bf16[512,64,128]{2,0,1:T(8,128)(2,1)S(1)}, bf16[512,64,128]{2,0,1:T(8,128)(2,1)S(1)}) fusion(bf16[2,512,64,128]{3,1,2,0:T(8,128)(2,1)} %all-gather.2.cloned.1.call-done), kind=kLoop, calls=%fused_computation.9 | loop fusion | bytes 33554432 | tf_op jit(solution)/shard_map/squeeze | solution.py:97
  611.1 4.2 fusion.17
  615.3 1.0 copy.35
  616.2 4.2 fusion.23
  620.4 1.0 copy.34
  (17 shorter events, 0.1 us)
Async XLA Ops:
  7.2 577.9 %copy-start = (f32[64,512]{1,0:T(8,128)S(1)}, f32[64,512]{1,0:T(8,128)}, u32[]{:S(2)}) copy-start(f32[64,512]{1,0:T(8,128)} %param.10) | copy-start | bytes 393220
  7.2 597.3 %all-gather.2.cloned.1.call-start = ((), (), s32[]{:S(2)}) async-start(), calls=%async_computation.1 | async-start | bytes 20971520 | tf_op jit(solution)/shard_map/all_gather | solution.py:131
  209.9 8.5 %copy-start.3 = (f32[1,16,512]{2,1,0:T(8,128)S(1)}, f32[1,16,512]{2,1,0:T(8,128)}, u32[]{:S(2)}) copy-start(f32[1,16,512]{2,1,0:T(8,128)} %param.9) | copy-start | bytes 98308
  209.9 8.7 %copy-start.4 = (s32[4]{0:T(128)S(1)}, s32[4]{0:T(128)}, u32[]{:S(2)}) copy-start(s32[4]{0:T(128)} %param.13) | copy-start | bytes 52
  209.9 10.0 %copy-start.1 = (s32[512]{0:T(512)S(1)}, s32[512]{0:T(512)}, u32[]{:S(2)}) copy-start(s32[512]{0:T(512)} %param.11) | copy-start | bytes 6148
  209.9 374.5 %copy-start.2 = (s32[64]{0:T(128)S(1)}, s32[64]{0:T(128)}, u32[]{:S(2)}) copy-start(s32[64]{0:T(128)} %param.12) | copy-start | bytes 772
Sparse Core Ops, SparseCore 0:
  218.5 152.3 all-gather.1
where the time goes:
time: 629 us; the launch traced here: 628 us
  blocking collectives  468 us (74%)
  local copies, waits for them, and re-layouts  77.8 us (12%)
  other arithmetic  53.3 us (8%)
  between operations  14.9 us (2%)
  matrix products  13.9 us (2%)
    psum x1, blocking collectives, from_root(): return lax.psum(kept, axis)  360 us
    all_to_all x1, blocking collectives, on_device(): lax.all_to_all(spectra, 'stn', split_axis=2, concat_axis=1, tiled=True)  108 us
    convert_element_type x1, other arithmetic, channelize(): filtered.astype(jnp.bfloat16)  28.3 us
    another operation x3, local copies, waits for them, and re-layouts, channelize(): return jnp.stack((chan_re, chan_im), axis=0)  23.4 us
  transfers between devices with their start and end apart: 1, of which 0 were waited for; matrix products, arithmetic and copies ran while one was open for 4% of the time, Pallas kernels for 0%

commit v1 on v0

--- a/solution.py
+++ b/solution.py
@@ -12,7 +12,7 @@
 
 def from_root(value, axis, source):
     kept = jnp.where(lax.axis_index(axis) == source, value, 0).astype(value.dtype)
-    return lax.psum(kept, axis)
+    return jnp.sum(lax.all_gather(kept, axis), axis=0)
 
 
 def dft_tables():

time: 629 us -> 428 us (0.68)
  blocking collectives: 468 us -> 0 us
  waiting for transfers between devices: 0.02 us -> 243 us
  starting transfers between devices: 0.04 us -> 14.8 us
    psum x1 -> x0, blocking collectives: 360 us -> none  [from_root(): return lax.psum(kept, axis)]
    all_gather x1, waiting for transfers between devices: 0.01 us -> 133 us  [on_device(): lax.all_gather(lax.all_to_all(spectra, 'stn', split_axis=2, concat_axis=1...]
    all_to_all x1 -> x0, blocking collectives: 108 us -> none  [on_device(): lax.all_to_all(spectra, 'stn', split_axis=2, concat_axis=1, tiled=True)]
    all_to_all x0 -> x1, waiting for transfers between devices: none -> 94.1 us  [on_device(): lax.all_to_all(spectra, 'stn', split_axis=2, concat_axis=1, tiled=True)]
    all_gather x0 -> x1, waiting for transfers between devices: none -> 16 us  [from_root(): return jnp.sum(lax.all_gather(kept, axis), axis=0)]
    all_to_all x0 -> x1, starting transfers between devices: none -> 14.7 us  [on_device(): lax.all_to_all(spectra, 'stn', split_axis=2, concat_axis=1, tiled=True)]
  transfers between devices with their start and end apart: 1 -> 3, of which waited for: 0 -> 3; matrix products, arithmetic and copies ran while one was open for 4% -> 10% of each run, Pallas kernels for 0% -> 0%
where the time goes in v1:
time: 428 us; the launch traced here: 423 us
  waiting for transfers between devices  243 us (57%)
  local copies, waits for them, and re-layouts  80.4 us (19%)
  other arithmetic  56.4 us (13%)
  between operations  15 us (4%)
  starting transfers between devices  14.8 us (3%)
  matrix products  14 us (3%)
    all_gather x1, waiting for transfers between devices, on_device(): lax.all_gather(lax.all_to_all(spectra, 'stn', split_axis=2, concat_axis=1...  133 us
    all_to_all x1, waiting for transfers between devices, on_device(): lax.all_to_all(spectra, 'stn', split_axis=2, concat_axis=1, tiled=True)  94.1 us
    convert_element_type x1, other arithmetic, channelize(): filtered.astype(jnp.bfloat16)  29.1 us
    another operation x3, local copies, waits for them, and re-layouts, channelize(): return jnp.stack((chan_re, chan_im), axis=0)  23.4 us
    all_gather x1, waiting for transfers between devices, from_root(): return jnp.sum(lax.all_gather(kept, axis), axis=0)  16 us
    all_to_all x1, starting transfers between devices, on_device(): lax.all_to_all(spectra, 'stn', split_axis=2, concat_axis=1, tiled=True)  14.7 us
    all_to_all x2, local copies, waits for them, and re-layouts, on_device(): lax.all_to_all(spectra, 'stn', split_axis=2, concat_axis=1, tiled=True)  13.4 us
    slice x2, local copies, waits for them, and re-layouts, channelize(): second[:, :half_q].astype(jnp.bfloat16)  10.6 us
  transfers between devices with their start and end apart: 3, of which 3 were waited for; matrix products, arithmetic and copies ran while one was open for 10% of the time, Pallas kernels for 0%

profile of v1, /device:TPU:16, one launch (start us, length us, event | category | flops | bytes accessed | tf_op | source)
XLA Modules:
  0.0 423.3 jit_solution(3262116013972345560)
XLA Ops:
  7.2 0.1 cosine_convert_fusion.1
  7.3 0.1 fusion.46
  7.5 0.1 fusion.41
  7.6 0.3 sine_convert_fusion
  7.9 0.3 fusion.49
  8.2 2.6 fusion.59
  10.8 6.3 %reshape.168 = bf16[2,2,75,8192]{3,2,1,0:T(8,128)(2,1)} reshape(bf16[2,2,614400]{2,1,0:T(2,128)(2,1)} %param.7) | data formatting | bytes 9830400 | tf_op jit(solution)/shard_map/reshape | solution.py:57
  17.1 29.1 %add_convert_fusion.1 = bf16[2,2,64,8192]{3,2,1,0:T(8,128)(2,1)S(1)} fusion(bf16[2,2,75,8192]{3,2,1,0:T(8,128)(2,1)} %reshape.168, f32[8192]{0:T(1024)S(1)} %bitcast.81, f32[8192]{0:T(1024)S(1)} %bitcast.82, f32[8192]{0:T(1024)S(1)} %bitcast.72, f32[8192]{0:T(1024)S(1)} %bitcast.73, f32[8192]{0:T(1024)S(1)} %bitcast.74, f32[8192]{0:T(1024)S(1)} %bitcast.75, ...), kind=kLoop, calls=%fused_computation.16 | loop fusion | flops 75497472 | bytes 54919168 | tf_op jit(solution)/shard_map/convert_element_type | solution.py:63
  46.2 1.2 copy.36
  47.4 2.5 convolution_bitcast_fusion
  49.8 2.5 add_convert_fusion
  52.3 3.1 convert_bitcast_fusion
  55.5 4.3 %fusion.58 = (bf16[2,64,64,2,64]{1,2,4,3,0:T(8,128)(2,1)}, bf16[2,64,64,2,64]{1,2,4,3,0:T(8,128)(2,1)}) fusion(bf16[2,128,64,2,64]{1,2,4,3,0:T(8,128)(2,1)S(1)} %convert_bitcast_fusion), kind=kLoop, calls=%fused_computation.94 | loop fusion | bytes 8388608 | tf_op jit(solution)/shard_map/slice | solution.py:84
  59.7 6.3 %copy.23 = bf16[2,64,64,2,64]{2,1,4,3,0:T(8,128)(2,1)} copy(bf16[2,64,64,2,64]{1,2,4,3,0:T(8,128)(2,1)} %get-tuple-element.12) | data formatting | bytes 4194304 | tf_op jit(solution)/shard_map/slice | solution.py:84
  66.1 5.7 %stack_reshape.6 = bf16[1,2,4096,128]{2,3,1,0:T(8,128)(2,1)S(1)} reshape(bf16[2,64,64,2,64]{2,1,4,3,0:T(8,128)(2,1)} %copy.23) | data formatting | bytes 4194304 | tf_op jit(solution)/shard_map/stack;reshape | solution.py:93
  71.7 6.3 %copy.24 = bf16[2,64,64,2,64]{2,1,4,3,0:T(8,128)(2,1)} copy(bf16[2,64,64,2,64]{1,2,4,3,0:T(8,128)(2,1)} %get-tuple-element.13) | data formatting | bytes 4194304 | tf_op jit(solution)/shard_map/slice | solution.py:89
  78.1 6.6 %stack_reshape.7 = bf16[1,2,4096,128]{2,3,1,0:T(8,128)(2,1)} reshape(bf16[2,64,64,2,64]{2,1,4,3,0:T(8,128)(2,1)} %copy.24) | data formatting | bytes 4194304 | tf_op jit(solution)/shard_map/stack;reshape | solution.py:93
  84.7 3.9 pad_maximum_fusion.3
  88.6 11.2 %copy.25 = bf16[2,2,4096,128]{3,1,0,2:T(2,128)(2,1)} copy(bf16[2,2,4096,128]{2,3,1,0:T(8,128)(2,1)} %pad_maximum_fusion.3) | data formatting | bytes 8388608 | tf_op jit(solution)/shard_map/stack | solution.py:93
  99.8 14.7 %all-to-all-start = ((bf16[2,2,4096,128]{3,1,0,2:T(2,128)(2,1)}), bf16[2,2,4096,128]{3,1,0,2:T(2,128)(2,1)}, u32[]{:S(2)}, u32[]{:S(2)}) async-start(bf16[2,2,4096,128]{3,1,0,2:T(2,128)(2,1)} %copy.25), calls=%async_computation | async-start | bytes 8388608 | tf_op jit(solution)/shard_map/all_to_all | solution.py:132
  114.6 0.0 all-gather.6.cloned.1.call-start
  114.6 0.6 dynamic_slice.3
  115.9 0.6 broadcast_select_fusion
  116.5 0.0 all-gather.6.cloned.1.call-update
  116.5 0.0 all-gather.4.cloned.1.call-start
  116.6 94.1 %all-to-all-done = bf16[2,2,4096,128]{3,1,0,2:T(2,128)(2,1)} async-done(((bf16[2,2,4096,128]{3,1,0,2:T(2,128)(2,1)}), bf16[2,2,4096,128]{3,1,0,2:T(2,128)(2,1)}, u32[]{:S(2)}, u32[]{:S(2)}) %all-to-all-start) | async-done | bytes 4194336 | tf_op jit(solution)/shard_map/all_to_all | solution.py:132
  210.7 4.7 %copy.26 = bf16[2,2,4096,128]{3,2,1,0:T(8,128)(2,1)} copy(bf16[2,2,4096,128]{3,1,0,2:T(2,128)(2,1)} %all-to-all-done) | data formatting | bytes 8388608 | tf_op jit(solution)/shard_map/all_to_all | solution.py:132
  215.4 8.6 %copy.27 = bf16[2,64,2,64,128]{4,2,1,3,0:T(2,128)(2,1)} copy(bf16[2,64,2,64,128]{4,3,1,2,0:T(8,128)(2,1)} %bitcast.67) | data formatting | bytes 8388608 | tf_op jit(solution)/shard_map/all_to_all | solution.py:132
  224.0 0.0 all-gather.4.cloned.1.call-update
  224.1 0.7 gather_fusion
  224.8 0.6 gather_fusion.1
  225.4 0.1 copy.28
  225.6 3.7 gather_fusion.2
  229.3 1.0 gather_fusion.3
  230.4 0.1 copy.29
  230.5 16.0 %all-gather.6.cloned.1.call-done = f32[64,16,512]{2,1,0:T(8,128)} async-done(((f32[1,16,512]{2,1,0:T(8,128)}), f32[64,16,512]{2,1,0:T(8,128)}) %all-gather.6.cloned.1.call-update) | async-done | bytes 2097168 | tf_op jit(solution)/shard_map/all_gather | solution.py:15
  246.5 1.7 reduce.1
  248.2 0.1 copy.30
  248.3 1.0 gather_fusion.4
  249.4 0.1 copy.31
  249.5 8.3 %fusion.57 = bf16[16,512,64]{1,0,2:T(8,128)(2,1)} fusion(f32[64]{0:T(128)S(1)} %add_convert_fusion.2, f32[16,512]{1,0:T(8,128)S(1)} %copy.31, f32[16,512]{1,0:T(8,128)S(1)} %copy.29), kind=kLoop, calls=%fused_computation.93 | loop fusion | flops 4194304 | bytes 1114368 | tf_op jit(solution)/shard_map/neg | solution.py:47
  257.8 9.2 %negate_convert_fusion = (bf16[16,512,64]{1,0,2:T(8,128)(2,1)}, bf16[16,512,64]{1,0,2:T(8,128)(2,1)}) fusion(f32[64]{0:T(128)S(1)} %add_convert_fusion.2, f32[16,512]{1,0:T(8,128)S(1)} %copy.31, f32[16,512]{1,0:T(8,128)S(1)} %copy.29), kind=kLoop, calls=%fused_computation.26 | loop fusion | flops 3670016 | bytes 2162944 | tf_op jit(solution)/shard_map/convert_element_type | solution.py:46
  267.0 132.5 %all-gather.4.cloned.1.call-done = bf16[2,512,64,128]{3,1,2,0:T(8,128)(2,1)} async-done(((bf16[2,128,64,128]{3,1,2,0:T(8,128)(2,1)}), bf16[2,512,64,128]{3,1,2,0:T(8,128)(2,1)}) %all-gather.4.cloned.1.call-update) | async-done | bytes 16777232 | tf_op jit(solution)/shard_map/all_gather | solution.py:131
  399.5 6.6 %slice_bitcast_fusion.1 = (bf16[512,64,128]{2,0,1:T(8,128)(2,1)S(1)}, bf16[512,64,128]{2,0,1:T(8,128)(2,1)S(1)}) fusion(bf16[2,512,64,128]{3,1,2,0:T(8,128)(2,1)} %all-gather.4.cloned.1.call-done), kind=kLoop, calls=%fused_computation.9 | loop fusion | bytes 33554432 | tf_op jit(solution)/shard_map/squeeze | solution.py:97
  406.1 4.2 fusion.17
  410.3 1.0 copy.33
  411.3 4.2 fusion.23
  415.5 1.0 copy.32
  (23 shorter events, 0.1 us)
Async XLA Ops:
  7.2 217.6 %copy-start = (f32[64,512]{1,0:T(8,128)S(1)}, f32[64,512]{1,0:T(8,128)}, u32[]{:S(2)}) copy-start(f32[64,512]{1,0:T(8,128)} %param.10) | copy-start | bytes 393220
  88.6 26.0 %copy-start.5 = (s32[4]{0:T(128)S(1)}, s32[4]{0:T(128)}, u32[]{:S(2)}) copy-start(s32[4]{0:T(128)} %param.13) | copy-start | bytes 52
  88.6 27.2 %copy-start.4 = (f32[1,16,512]{2,1,0:T(8,128)S(1)}, f32[1,16,512]{2,1,0:T(8,128)}, u32[]{:S(2)}) copy-start(f32[1,16,512]{2,1,0:T(8,128)} %param.9) | copy-start | bytes 98308
  99.8 110.9 %all-to-all-start = ((bf16[2,2,4096,128]{3,1,0,2:T(2,128)(2,1)}), bf16[2,2,4096,128]{3,1,0,2:T(2,128)(2,1)}, u32[]{:S(2)}, u32[]{:S(2)}) async-start(bf16[2,2,4096,128]{3,1,0,2:T(2,128)(2,1)} %copy.25), calls=%async_computation | async-start | bytes 8388608 | tf_op jit(solution)/shard_map/all_to_all | solution.py:132
  114.6 131.9 %all-gather.6.cloned.1.call-start = ((), (), s32[]{:S(2)}) async-start(), calls=%async_computation.2 | async-start | bytes 2129920 | tf_op jit(solution)/shard_map/all_gather | solution.py:15
  116.5 283.0 %all-gather.4.cloned.1.call-start = ((), (), s32[]{:S(2)}) async-start(), calls=%async_computation.1 | async-start | bytes 20971520 | tf_op jit(solution)/shard_map/all_gather | solution.py:131
  215.4 8.7 %copy-start.3 = (s32[64]{0:T(128)S(1)}, s32[64]{0:T(128)}, u32[]{:S(2)}) copy-start(s32[64]{0:T(128)} %param.12) | copy-start | bytes 772
  215.4 10.2 %copy-start.2 = (s32[512]{0:T(512)S(1)}, s32[512]{0:T(512)}, u32[]{:S(2)}) copy-start(s32[512]{0:T(512)} %param.11) | copy-start | bytes 6148
  411.3 5.2 %copy-start.1 = (f32[64,512]{1,0:T(8,128)S(1)}, f32[64,512]{1,0:T(8,128)}, u32[]{:S(2)}) copy-start(f32[64,512]{1,0:T(8,128)} %param.10) | copy-start | bytes 393220
Sparse Core Ops, SparseCore 0:
  119.5 126.9 all-gather.5
  248.3 151.1 all-gather.3
